TPU v7x, 32 devices: a whole 2x2x4 slice. The times are simulated.
32 devices in a mesh: pole: 2 (over x), row: 8 (over z, y), col: 2 (over core).
Axes of the slice: x: 2, y: 2, z: 4, core: 2. Of those that a mesh axis runs over, the one named last changes fastest.
Arguments:
- ancestor_inverse: float32 [2, 24576, 12288], P(None, ('pole', 'row'), 'col'), parts along dimension 1, may hold values from -6 to 6
- factor_panels: float32 [4, 2, 24576, 128], P(None, None, ('pole', 'col', 'row')), parts along dimension 2, may hold values from -0.0546875 to 0.0546875
- diag_inverse: float32 [8, 2, 128, 128], P('pole'), parts along dimension 0, may hold values from -6 to 6
- coupling: float32 [4, 2, 128, 128], P('pole'), parts along dimension 0, may hold values from -0.5 to 0.5
- block_pattern: int32 [4, 96], replicated, may hold values from 0 to 1, as said below
- tree_order: int32 [4], replicated, may hold values from 0 to 3, each once
Outputs:
- inverse_panels: float32 [4, 2, 24576, 128], P(None, None, ('pole', 'row')), parts along dimension 2
- inverse_diagonal: float32 [8, 2, 128, 128], P('pole'), parts along dimension 0
- inverse_coupling: float32 [4, 2, 128, 128], P('pole'), parts along dimension 0
There are 2 independent parts, one for each index of `pole`. A program takes and returns all parts, laid end to end along the dimension named above; an argument that names none is the same for every part. Nothing has to cross between parts.
Inputs may be any that keep to these rules, and one draw needn't show every extreme that they name: `tree_order`: each supernode number appears once. `block_pattern`: blocks 0 and 48 lie in every supernode's structure.
All inputs are finite; a program needn't handle non-finite values.
Results may differ from a plain program's by a relative error of at most 0.0001.
Values sent between devices are 32-bit elements; how exact they have to be, the bound alone decides.
A program may use at most 192 MiB of HBM per device.

v0:
```python
import jax
import jax.numpy as jnp
from jax import lax
from jax.sharding import PartitionSpec as P


def swapped(block, axis, bit):
    count = lax.axis_size(axis)
    route = []
    for low in range(count):
        high = low | 1 << bit
        if high != low and high < count:
            route += [(low, high), (high, low)]
    return lax.ppermute(block, axis, route)


def matmul(left_side, right_side):
    return jnp.dot(
        left_side, right_side, preferred_element_type=jnp.float32, precision=lax.Precision.HIGHEST
    )


def multiply(left_side, right_side):
    real_part = matmul(left_side[0], right_side[0]) - matmul(left_side[1], right_side[1])
    imag_part = matmul(left_side[0], right_side[1]) + matmul(left_side[1], right_side[0])
    return jnp.stack([real_part, imag_part])


def flipped(matrix):
    return jnp.swapaxes(matrix, 1, 2)


def row_masks(pattern_eff, first_row, row_count, block_rows):
    row_index = first_row + jnp.arange(row_count, dtype=jnp.int32)
    blocks = row_index // block_rows
    onehot = (blocks[:, None] == jnp.arange(pattern_eff.shape[1], dtype=jnp.int32)[None, :]).astype(
        jnp.float32
    )
    return matmul(pattern_eff, onehot.T)


def per_device(ancestor_inverse, factor_panels, diag_inverse, coupling, block_pattern, tree_order):
    grid_row = lax.axis_index("row")
    grid_col = lax.axis_index("col")
    tile_rows = ancestor_inverse.shape[1]
    half_rows = ancestor_inverse.shape[2]
    piece_rows = factor_panels.shape[2]
    block_rows = factor_panels.shape[3]
    super_count = factor_panels.shape[0]
    share_rows = tile_rows // 2
    sorted_pattern = jnp.take(block_pattern, tree_order, axis=0).astype(jnp.float32)
    pattern_eff = jnp.concatenate(
        [sorted_pattern[:2], sorted_pattern[2:] * sorted_pattern[:2]], axis=0
    )
    source_mask = row_masks(
        pattern_eff, grid_col * half_rows + grid_row * piece_rows, piece_rows, block_rows
    )
    target_mask = row_masks(pattern_eff, grid_row * tile_rows, tile_rows, block_rows)
    panels = jnp.take(factor_panels, tree_order, axis=0) * source_mask[:, None, :, None]
    diag_blocks = jnp.take(diag_inverse, tree_order, axis=0)
    columns = []
    products = []
    for tree_slot in range(super_count):
        gathered = lax.all_gather(panels[tree_slot], "row", axis=1, tiled=True)
        columns.append(gathered)
        products.append(lax.psum(multiply(ancestor_inverse, gathered), "col"))
    own_flag = (grid_row * tile_rows // half_rows == grid_col).astype(jnp.float32)
    offset = jnp.clip(grid_row * tile_rows - grid_col * half_rows, 0, half_rows - tile_rows)
    own_windows = jnp.stack(
        [
            lax.dynamic_slice_in_dim(column_set, offset, tile_rows, 1) * own_flag
            for column_set in columns
        ]
    )
    partner_windows = swapped(own_windows, "col", 0)
    tile_windows = own_windows + partner_windows

    def share(matrix):
        return lax.dynamic_slice_in_dim(matrix, grid_col * share_rows, share_rows, 1)

    windows = [share(tile_windows[tree_slot]) for tree_slot in range(super_count)]
    parent_cols = [
        -target_mask[tree_slot][None, :, None] * products[tree_slot] for tree_slot in range(2)
    ]
    child_cols = [
        -target_mask[tree_slot + 2][None, :, None]
        * (products[tree_slot + 2] + multiply(parent_cols[tree_slot], coupling[tree_slot]))
        for tree_slot in range(2)
    ]
    parent_local = [
        multiply(flipped(windows[tree_slot]), share(parent_cols[tree_slot]))
        for tree_slot in range(2)
    ]
    cross_local = [
        multiply(flipped(share(parent_cols[tree_slot])), windows[tree_slot + 2])
        for tree_slot in range(2)
    ]
    child_local = [
        multiply(flipped(windows[tree_slot + 2]), share(child_cols[tree_slot]))
        for tree_slot in range(2)
    ]
    parent_sums = lax.psum(jnp.stack(parent_local), ("row", "col"))
    parent_diag = [diag_blocks[tree_slot] - parent_sums[tree_slot] for tree_slot in range(2)]
    child_totals = lax.psum(jnp.stack(cross_local + child_local), ("row", "col"))
    crosses = [
        -(child_totals[tree_slot] + multiply(parent_diag[tree_slot], coupling[tree_slot]))
        for tree_slot in range(2)
    ]
    child_sums = [child_totals[2 + tree_slot] for tree_slot in range(2)]
    child_diag = [
        diag_blocks[tree_slot + 2]
        - child_sums[tree_slot]
        - multiply(flipped(coupling[tree_slot]), crosses[tree_slot])
        for tree_slot in range(2)
    ]
    all_cols = jnp.stack(parent_cols + child_cols)
    all_diag = jnp.stack(parent_diag + child_diag)
    inverse_panels = jnp.zeros_like(all_cols).at[tree_order].set(all_cols)
    inverse_diagonal = jnp.zeros_like(all_diag).at[tree_order].set(all_diag)
    return (inverse_panels, inverse_diagonal, jnp.stack(crosses))


def solution(mesh):
    return jax.shard_map(
        per_device,
        mesh=mesh,
        in_specs=(
            P(None, ("pole", "row"), "col"),
            P(None, None, ("pole", "col", "row"), None),
            P("pole", None, None, None),
            P("pole", None, None, None),
            P(),
            P(),
        ),
        out_specs=(
            P(None, None, ("pole", "row"), None),
            P("pole", None, None, None),
            P("pole", None, None, None),
        ),
        check_vma=False,
    )
```

profile of v0, /device:TPU:0, one launch (start us, length us, event | category | flops | bytes accessed | tf_op | source)
XLA Modules:
  0.0 873.5 jit_solution(7536772676169645142)
XLA Ops:
  10.7 2.4 gather_fusion.1
  13.5 2.4 select_multiply_fusion
  19.7 99.5 %all-gather.11.cloned.1.call-done = f32[1,2,6144,128]{3,2,1,0:T(8,128)} async-done(((f32[1,2,768,128]{3,2,1,0:T(8,128)}), f32[1,2,6144,128]{3,2,1,0:T(8,128)}) %all-gather.11.cloned.1.call-update) | async-done | bytes 6291472 | tf_op jit(solution)/shard_map/all_gather | solution.py:64
  119.2 36.1 %fusion.8 = f32[128,1536]{1,0:T(8,128)S(1)} fusion(f32[2,1536,6144]{2,1,0:T(8,128)} %param.6, f32[1,2,6144,128]{3,2,1,0:T(8,128)} %all-gather.11.cloned.1.call-done), kind=kOutput, calls=%fused_computation.13 | convolution fusion | flops 14495514624 | bytes 41680896 | tf_op jit(solution)/shard_map/dot_general | solution.py:18
  155.3 35.0 %fusion.10 = f32[128,1536]{1,0:T(8,128)S(1)} fusion(f32[2,1536,6144]{2,1,0:T(8,128)} %param.6, f32[1,2,6144,128]{3,2,1,0:T(8,128)S(1)} %copy-done.2), kind=kOutput, calls=%fused_computation.15 | convolution fusion | flops 14495514624 | bytes 41680896 | tf_op jit(solution)/shard_map/dot_general | solution.py:18
  190.3 35.3 %fusion.73 = f32[1,1536,128]{1,2,0:T(8,128)S(1)} fusion(f32[128,1536]{1,0:T(8,128)S(1)} %fusion.8, f32[2,1536,6144]{2,1,0:T(8,128)} %param.6, f32[1,2,6144,128]{3,2,1,0:T(8,128)S(1)} %copy-done.2), kind=kOutput, calls=%fused_computation.79 | convolution fusion | flops 14495711232 | bytes 42467328 | tf_op jit(solution)/shard_map/dot_general | solution.py:18
  225.6 35.6 %fusion.67 = f32[1,1536,128]{1,2,0:T(8,128)S(1)} fusion(f32[128,1536]{1,0:T(8,128)S(1)} %fusion.10, f32[2,1536,6144]{2,1,0:T(8,128)} %param.6, f32[1,2,6144,128]{3,2,1,0:T(8,128)S(1)} %copy-done.2), kind=kOutput, calls=%fused_computation.77 | convolution fusion | flops 14495711232 | bytes 42467328 | tf_op jit(solution)/shard_map/dot_general | solution.py:18
  261.3 36.6 %fusion.4 = f32[128,1536]{1,0:T(8,128)S(1)} fusion(f32[2,1536,6144]{2,1,0:T(8,128)} %param.6, f32[1,2,6144,128]{3,2,1,0:T(8,128)} %all-gather.13.cloned.1.call-done), kind=kOutput, calls=%fused_computation.9 | convolution fusion | flops 14495514624 | bytes 41680896 | tf_op jit(solution)/shard_map/dot_general | solution.py:18
  297.9 35.2 %fusion.6 = f32[128,1536]{1,0:T(8,128)S(1)} fusion(f32[2,1536,6144]{2,1,0:T(8,128)} %param.6, f32[1,2,6144,128]{3,2,1,0:T(8,128)S(1)} %copy-done.3), kind=kOutput, calls=%fused_computation.11 | convolution fusion | flops 14495514624 | bytes 41680896 | tf_op jit(solution)/shard_map/dot_general | solution.py:18
  334.4 35.2 %fusion.85 = f32[1,1536,128]{1,2,0:T(8,128)S(1)} fusion(f32[128,1536]{1,0:T(8,128)S(1)} %fusion.4, f32[2,1536,6144]{2,1,0:T(8,128)} %param.6, f32[1,2,6144,128]{3,2,1,0:T(8,128)S(1)} %copy-done.3), kind=kOutput, calls=%fused_computation.83 | convolution fusion | flops 14495711232 | bytes 42467328 | tf_op jit(solution)/shard_map/dot_general | solution.py:18
  369.6 35.0 %fusion.79 = f32[1,1536,128]{1,2,0:T(8,128)S(1)} fusion(f32[128,1536]{1,0:T(8,128)S(1)} %fusion.6, f32[2,1536,6144]{2,1,0:T(8,128)} %param.6, f32[1,2,6144,128]{3,2,1,0:T(8,128)S(1)} %copy-done.3), kind=kOutput, calls=%fused_computation.81 | convolution fusion | flops 14495711232 | bytes 42467328 | tf_op jit(solution)/shard_map/dot_general | solution.py:18
  405.9 36.3 %fusion = f32[128,1536]{1,0:T(8,128)S(1)} fusion(f32[2,1536,6144]{2,1,0:T(8,128)} %param.6, f32[1,2,6144,128]{3,2,1,0:T(8,128)} %all-gather.15.cloned.1.call-done), kind=kOutput, calls=%fused_computation.5 | convolution fusion | flops 14495514624 | bytes 41680896 | tf_op jit(solution)/shard_map/dot_general | solution.py:18
  442.3 35.0 %fusion.2 = f32[128,1536]{1,0:T(8,128)S(1)} fusion(f32[2,1536,6144]{2,1,0:T(8,128)} %param.6, f32[1,2,6144,128]{3,2,1,0:T(8,128)S(1)} %copy-done.4), kind=kOutput, calls=%fused_computation.7 | convolution fusion | flops 14495514624 | bytes 41680896 | tf_op jit(solution)/shard_map/dot_general | solution.py:18
  477.3 35.5 %fusion.97 = f32[1,1536,128]{1,2,0:T(8,128)S(1)} fusion(f32[128,1536]{1,0:T(8,128)S(1)} %fusion, f32[2,1536,6144]{2,1,0:T(8,128)} %param.6, f32[1,2,6144,128]{3,2,1,0:T(8,128)S(1)} %copy-done.4), kind=kOutput, calls=%fused_computation.87 | convolution fusion | flops 14495711232 | bytes 42467328 | tf_op jit(solution)/shard_map/dot_general | solution.py:18
  512.8 35.0 %fusion.91 = f32[1,1536,128]{1,2,0:T(8,128)S(1)} fusion(f32[128,1536]{1,0:T(8,128)S(1)} %fusion.2, f32[2,1536,6144]{2,1,0:T(8,128)} %param.6, f32[1,2,6144,128]{3,2,1,0:T(8,128)S(1)} %copy-done.4), kind=kOutput, calls=%fused_computation.85 | convolution fusion | flops 14495711232 | bytes 42467328 | tf_op jit(solution)/shard_map/dot_general | solution.py:18
  549.1 36.3 %fusion.12 = f32[128,1536]{1,0:T(8,128)S(1)} fusion(f32[2,1536,6144]{2,1,0:T(8,128)} %param.6, f32[1,2,6144,128]{3,2,1,0:T(8,128)} %all-gather.9.cloned.1.call-done), kind=kOutput, calls=%fused_computation.17 | convolution fusion | flops 14495514624 | bytes 41680896 | tf_op jit(solution)/shard_map/dot_general | solution.py:18
  585.4 35.0 %fusion.14 = f32[128,1536]{1,0:T(8,128)S(1)} fusion(f32[2,1536,6144]{2,1,0:T(8,128)} %param.6, f32[1,2,6144,128]{3,2,1,0:T(8,128)S(1)} %copy-done.5), kind=kOutput, calls=%fused_computation.19 | convolution fusion | flops 14495514624 | bytes 41680896 | tf_op jit(solution)/shard_map/dot_general | solution.py:18
  620.5 35.5 %fusion.61 = f32[1,1536,128]{1,2,0:T(8,128)S(1)} fusion(f32[128,1536]{1,0:T(8,128)S(1)} %fusion.12, f32[2,1536,6144]{2,1,0:T(8,128)} %param.6, f32[1,2,6144,128]{3,2,1,0:T(8,128)S(1)} %copy-done.5), kind=kOutput, calls=%fused_computation.75 | convolution fusion | flops 14495711232 | bytes 42467328 | tf_op jit(solution)/shard_map/dot_general | solution.py:18
  655.9 35.0 %fusion.55 = f32[1,1536,128]{1,2,0:T(8,128)S(1)} fusion(f32[128,1536]{1,0:T(8,128)S(1)} %fusion.14, f32[2,1536,6144]{2,1,0:T(8,128)} %param.6, f32[1,2,6144,128]{3,2,1,0:T(8,128)S(1)} %copy-done.5), kind=kOutput, calls=%fused_computation.73 | convolution fusion | flops 14495711232 | bytes 42467328 | tf_op jit(solution)/shard_map/dot_general | solution.py:18
  694.0 2.2 dynamic-slice_multiply_fusion.1
  696.2 2.3 dynamic-slice_multiply_fusion
  698.5 2.5 dynamic-slice_multiply_fusion.3
  701.1 2.9 pad_maximum_fusion.1
  704.5 1.7 gather_fusion.2
  709.7 13.4 %all-reduce.7.cloned.1.call-done = (f32[2,1536,128]{1,2,0:T(8,128)}, f32[2,1536,128]{1,2,0:T(8,128)}, f32[2,1536,128]{1,2,0:T(8,128)}, f32[2,1536,128]{1,2,0:T(8,128)}) async-done(((f32[2,1536,128]{1,2,0:T(8,128)}, f32[2,1536,128]{1,2,0:T(8,128)}, f32[2,1536,128]{1,2,0:T(8,128)}, f32[2,1536,128]{1,2,0:T(8,128)}), (f32[2,1536,128]{1,2,0:T(8,128)}, f32[2,1536,128]{1,2,0:T(8,128)}, f32[2,1536,128]{1,2,0:T(8,128)}, ...) | async-done | bytes 6291472 | tf_op jit(solution)/shard_map/psum | solution.py:66
  732.7 3.3 fusion.220
  760.9 4.3 pad_maximum_fusion
  765.2 6.6 copy.33
  771.8 3.2 broadcast_in_dim.45
  775.0 13.3 %scatter_fusion = f32[4,2,1536,128]{3,2,1,0:T(8,128)} fusion(f32[4,2,1536,128]{3,2,1,0:T(8,128)} %broadcast_in_dim.45, s32[4]{0:T(128)S(1)} %copy-done.32, f32[4,2,1536,128]{3,2,1,0:T(8,128)} %copy.33), kind=kCustom, calls=%fused_computation.3 | custom fusion | bytes 18874384 | tf_op jit(solution)/shard_map/scatter | solution.py:118
  788.3 66.6 %all-reduce.5.cloned.1.call-done = (f32[4,2,128,128]{3,2,1,0:T(8,128)}, f32[2,2,128,128]{3,2,1,0:T(8,128)}) async-done(((f32[4,2,128,128]{3,2,1,0:T(8,128)}, f32[2,2,128,128]{3,2,1,0:T(8,128)}), (f32[4,2,128,128]{3,2,1,0:T(8,128)}, f32[2,2,128,128]{3,2,1,0:T(8,128)})) %all-reduce.5.cloned.1.call-update) | async-done | bytes 786448 | tf_op jit(solution)/shard_map/psum | solution.py:104
  863.6 2.7 scatter_fusion.1
  (183 shorter events, 60.8 us)
Async XLA Ops:
  7.2 3.5 copy-start
  7.2 112.0 %all-gather.11.cloned.1.call-start = ((), (), s32[]{:S(2)}) async-start(), calls=%async_computation.1 | async-start | bytes 7077888 | tf_op jit(solution)/shard_map/all_gather | solution.py:64
  8.0 5.4 copy-start.33
  9.3 3.8 copy-start.30
  17.6 243.7 %all-gather.13.cloned.1.call-start = ((), (), s32[]{:S(2)}) async-start(), calls=%async_computation.2 | async-start | bytes 7077888 | tf_op jit(solution)/shard_map/all_gather | solution.py:64
  18.3 387.6 %all-gather.15.cloned.1.call-start = ((), (), s32[]{:S(2)}) async-start(), calls=%async_computation.3 | async-start | bytes 7077888 | tf_op jit(solution)/shard_map/all_gather | solution.py:64
  19.1 530.0 %all-gather.9.cloned.1.call-start = ((), (), s32[]{:S(2)}) async-start(), calls=%async_computation | async-start | bytes 7077888 | tf_op jit(solution)/shard_map/all_gather | solution.py:64
  19.7 703.5 %all-reduce.7.cloned.1.call-start = ((), (), s32[]{:S(2)}) async-start(), calls=%async_computation.5 | async-start | bytes 12582912 | tf_op jit(solution)/shard_map/psum | solution.py:66
  119.2 36.1 %copy-start.2 = (f32[1,2,6144,128]{3,2,1,0:T(8,128)S(1)}, f32[1,2,6144,128]{3,2,1,0:T(8,128)}, u32[]{:S(2)}) copy-start(f32[1,2,6144,128]{3,2,1,0:T(8,128)} %all-gather.11.cloned.1.call-done) | copy-start | bytes 18874372
  261.3 36.6 %copy-start.3 = (f32[1,2,6144,128]{3,2,1,0:T(8,128)S(1)}, f32[1,2,6144,128]{3,2,1,0:T(8,128)}, u32[]{:S(2)}) copy-start(f32[1,2,6144,128]{3,2,1,0:T(8,128)} %all-gather.13.cloned.1.call-done) | copy-start | bytes 18874372
  405.9 36.3 %copy-start.4 = (f32[1,2,6144,128]{3,2,1,0:T(8,128)S(1)}, f32[1,2,6144,128]{3,2,1,0:T(8,128)}, u32[]{:S(2)}) copy-start(f32[1,2,6144,128]{3,2,1,0:T(8,128)} %all-gather.15.cloned.1.call-done) | copy-start | bytes 18874372
  549.1 36.3 %copy-start.5 = (f32[1,2,6144,128]{3,2,1,0:T(8,128)S(1)}, f32[1,2,6144,128]{3,2,1,0:T(8,128)}, u32[]{:S(2)}) copy-start(f32[1,2,6144,128]{3,2,1,0:T(8,128)} %all-gather.9.cloned.1.call-done) | copy-start | bytes 18874372
  692.3 162.6 %all-reduce.5.cloned.1.call-start = ((), (), s32[]{:S(2)}) async-start(), calls=%async_computation.4 | async-start | bytes 1572864 | tf_op jit(solution)/shard_map/psum | solution.py:104
  694.0 7.1 copy-start.10
  696.2 4.9 copy-start.12
  698.5 5.5 copy-start.14
  701.1 5.2 copy-start.35
  701.1 5.2 copy-start.37
  701.1 6.4 copy-start.18
  704.5 27.2 %collective-permute-start = (f32[4,2,1536,128]{3,2,1,0:T(8,128)}, f32[4,2,1536,128]{3,2,1,0:T(8,128)}, u32[]{:S(2)}, u32[]{:S(2)}) collective-permute-start(f32[4,2,1536,128]{3,2,1,0:T(8,128)} %pad_maximum_fusion.1), channel_id=1, source_target_pairs={{0,1},{1,0},{2,3},{3,2},{4,5},{5,4},{6,7},{7,6},{8,9},{9,8},{10,11... | collective-permute-start | bytes 18874376 | tf_op jit(solution)/shard_map/ppermute | solution.py:14
  725.3 3.4 copy-start.20
  728.8 3.5 copy-start.15
  728.8 3.9 copy-start.17
  746.2 9.5 %copy-start.8 = (f32[2,1536,128]{1,2,0:T(8,128)}, f32[2,1536,128]{1,2,0:T(8,128)S(1)}, u32[]{:S(2)}) copy-start(f32[2,1536,128]{1,2,0:T(8,128)S(1)} %get-tuple-element.36) | copy-start | bytes 4718596
  746.2 11.1 %copy-start.6 = (f32[2,1536,128]{1,2,0:T(8,128)}, f32[2,1536,128]{1,2,0:T(8,128)S(1)}, u32[]{:S(2)}) copy-start(f32[2,1536,128]{1,2,0:T(8,128)S(1)} %get-tuple-element.35) | copy-start | bytes 4718596
  757.3 3.5 copy-start.9
  775.0 79.9 %copy-start.21 = (f32[4,2,128,128]{3,2,1,0:T(8,128)S(1)}, f32[4,2,128,128]{3,2,1,0:T(8,128)}, u32[]{:S(2)}) copy-start(f32[4,2,128,128]{3,2,1,0:T(8,128)} %broadcast_select_fusion) | copy-start | bytes 1572868
  788.3 70.4 %copy-start.26 = (f32[2,128,128]{1,2,0:T(8,128)S(1)}, f32[2,128,128]{1,2,0:T(8,128)}, u32[]{:S(2)}) copy-start(f32[2,128,128]{1,2,0:T(8,128)} %get-tuple-element.31) | copy-start | bytes 393220
  854.9 5.0 copy-start.27
  854.9 6.2 copy-start.22
  854.9 6.2 copy-start.25
  859.9 6.4 copy-start.1
  (13 other events, 29.3 us)
Sparse Core Ops, SparseCore 0:
  17.7 101.4 all-gather.10
  121.4 96.8 all-gather.12
  220.5 96.9 all-gather.14
  320.1 96.8 all-gather.8
  692.4 30.6 all-reduce.6
  761.0 93.8 all-reduce.4
where the time goes:
time: 883 us; the launch traced here: 874 us
  matrix products  597 us (68%)
  waiting for transfers between devices  181 us (20%)
  other arithmetic  41.3 us (5%)
  local copies, waits for them, and re-layouts  38.3 us (4%)
  between operations  15.6 us (2%)
    dot_general x66, matrix products, matmul(): jnp.dot(left_side, right_side, preferred_element_type=jnp.float32, precis...  597 us
    all_gather x4, waiting for transfers between devices, per_device(): gathered = lax.all_gather(panels[tree_slot], 'row', axis=1, tiled=True)  99.5 us
    psum x1, waiting for transfers between devices, per_device(): lax.psum(jnp.stack(cross_local + child_local), ('row', 'col'))  66.6 us
  transfers between devices with their start and end apart: 7, of which 3 were waited for; matrix products, arithmetic and copies ran while one was open for 55% of the time, Pallas kernels for 0%

commit v1 on v0

--- a/solution.py
+++ b/solution.py
@@ -101,7 +101,7 @@
     ]
     parent_sums = lax.psum(jnp.stack(parent_local), ("row", "col"))
     parent_diag = [diag_blocks[tree_slot] - parent_sums[tree_slot] for tree_slot in range(2)]
-    child_totals = lax.psum(jnp.stack(cross_local + child_local), ("row", "col"))
+    child_totals = lax.psum(lax.psum(jnp.stack(cross_local + child_local), "row"), "col")
     crosses = [
         -(child_totals[tree_slot] + multiply(parent_diag[tree_slot], coupling[tree_slot]))
         for tree_slot in range(2)

time: 883 us -> 976 us (1.11)
  waiting for transfers between devices: 181 us -> 262 us
  matrix products: 597 us -> 610 us
    psum x1 -> x3, waiting for transfers between devices: 66.6 us -> 146 us  [the longest x1 74.5 us: per_device(): lax.psum(jnp.stack(cross_local + child_local), 'row')]
    dot_general x66, matrix products: 597 us -> 610 us  [matmul(): jnp.dot(left_side, right_side, preferred_element_type=jnp.float32, precis...]
  transfers between devices with their start and end apart: 7 -> 9, of which waited for: 3 -> 5; matrix products, arithmetic and copies ran while one was open for 55% -> 51% of each run, Pallas kernels for 0% -> 0%
where the time goes in v1:
time: 976 us; the launch traced here: 967 us
  matrix products  610 us (62%)
  waiting for transfers between devices  262 us (27%)
  other arithmetic  41 us (4%)
  local copies, waits for them, and re-layouts  38.2 us (4%)
  between operations  15.8 us (2%)
    dot_general x66, matrix products, matmul(): jnp.dot(left_side, right_side, preferred_element_type=jnp.float32, precis...  610 us
    all_gather x4, waiting for transfers between devices, per_device(): gathered = lax.all_gather(panels[tree_slot], 'row', axis=1, tiled=True)  99.5 us
    psum x1, waiting for transfers between devices, per_device(): lax.psum(jnp.stack(cross_local + child_local), 'row')  74.5 us
    psum x1, waiting for transfers between devices, per_device(): parent_sums = lax.psum(jnp.stack(parent_local), ('row', 'col'))  51.7 us
  transfers between devices with their start and end apart: 9, of which 5 were waited for; matrix products, arithmetic and copies ran while one was open for 51% of the time, Pallas kernels for 0%

profile of v1, /device:TPU:0, one launch (start us, length us, event | category | flops | bytes accessed | tf_op | source)
XLA Modules:
  0.0 967.0 jit_solution(15925034017285489864)
XLA Ops:
  10.7 2.4 gather_fusion.1
  13.5 2.4 select_multiply_fusion
  19.8 99.5 %all-gather.11.cloned.1.call-done = f32[1,2,6144,128]{3,2,1,0:T(8,128)} async-done(((f32[1,2,768,128]{3,2,1,0:T(8,128)}), f32[1,2,6144,128]{3,2,1,0:T(8,128)}) %all-gather.11.cloned.1.call-update) | async-done | bytes 6291472 | tf_op jit(solution)/shard_map/all_gather | solution.py:64
  119.2 36.1 %fusion.8 = f32[128,1536]{1,0:T(8,128)S(1)} fusion(f32[2,1536,6144]{2,1,0:T(8,128)} %param.6, f32[1,2,6144,128]{3,2,1,0:T(8,128)} %all-gather.11.cloned.1.call-done), kind=kOutput, calls=%fused_computation.13 | convolution fusion | flops 14495514624 | bytes 41680896 | tf_op jit(solution)/shard_map/dot_general | solution.py:18
  155.3 35.0 %fusion.10 = f32[128,1536]{1,0:T(8,128)S(1)} fusion(f32[2,1536,6144]{2,1,0:T(8,128)} %param.6, f32[1,2,6144,128]{3,2,1,0:T(8,128)S(1)} %copy-done.2), kind=kOutput, calls=%fused_computation.15 | convolution fusion | flops 14495514624 | bytes 41680896 | tf_op jit(solution)/shard_map/dot_general | solution.py:18
  190.4 35.3 %fusion.73 = f32[1,1536,128]{1,2,0:T(8,128)S(1)} fusion(f32[128,1536]{1,0:T(8,128)S(1)} %fusion.8, f32[2,1536,6144]{2,1,0:T(8,128)} %param.6, f32[1,2,6144,128]{3,2,1,0:T(8,128)S(1)} %copy-done.2), kind=kOutput, calls=%fused_computation.79 | convolution fusion | flops 14495711232 | bytes 42467328 | tf_op jit(solution)/shard_map/dot_general | solution.py:18
  225.7 35.6 %fusion.67 = f32[1,1536,128]{1,2,0:T(8,128)S(1)} fusion(f32[128,1536]{1,0:T(8,128)S(1)} %fusion.10, f32[2,1536,6144]{2,1,0:T(8,128)} %param.6, f32[1,2,6144,128]{3,2,1,0:T(8,128)S(1)} %copy-done.2), kind=kOutput, calls=%fused_computation.77 | convolution fusion | flops 14495711232 | bytes 42467328 | tf_op jit(solution)/shard_map/dot_general | solution.py:18
  261.3 36.5 %fusion.4 = f32[128,1536]{1,0:T(8,128)S(1)} fusion(f32[2,1536,6144]{2,1,0:T(8,128)} %param.6, f32[1,2,6144,128]{3,2,1,0:T(8,128)} %all-gather.13.cloned.1.call-done), kind=kOutput, calls=%fused_computation.9 | convolution fusion | flops 14495514624 | bytes 41680896 | tf_op jit(solution)/shard_map/dot_general | solution.py:18
  297.9 35.2 %fusion.6 = f32[128,1536]{1,0:T(8,128)S(1)} fusion(f32[2,1536,6144]{2,1,0:T(8,128)} %param.6, f32[1,2,6144,128]{3,2,1,0:T(8,128)S(1)} %copy-done.3), kind=kOutput, calls=%fused_computation.11 | convolution fusion | flops 14495514624 | bytes 41680896 | tf_op jit(solution)/shard_map/dot_general | solution.py:18
  334.4 35.2 %fusion.85 = f32[1,1536,128]{1,2,0:T(8,128)S(1)} fusion(f32[128,1536]{1,0:T(8,128)S(1)} %fusion.4, f32[2,1536,6144]{2,1,0:T(8,128)} %param.6, f32[1,2,6144,128]{3,2,1,0:T(8,128)S(1)} %copy-done.3), kind=kOutput, calls=%fused_computation.83 | convolution fusion | flops 14495711232 | bytes 42467328 | tf_op jit(solution)/shard_map/dot_general | solution.py:18
  369.6 35.1 %fusion.79 = f32[1,1536,128]{1,2,0:T(8,128)S(1)} fusion(f32[128,1536]{1,0:T(8,128)S(1)} %fusion.6, f32[2,1536,6144]{2,1,0:T(8,128)} %param.6, f32[1,2,6144,128]{3,2,1,0:T(8,128)S(1)} %copy-done.3), kind=kOutput, calls=%fused_computation.81 | convolution fusion | flops 14495711232 | bytes 42467328 | tf_op jit(solution)/shard_map/dot_general | solution.py:18
  405.9 36.3 %fusion = f32[128,1536]{1,0:T(8,128)S(1)} fusion(f32[2,1536,6144]{2,1,0:T(8,128)} %param.6, f32[1,2,6144,128]{3,2,1,0:T(8,128)} %all-gather.15.cloned.1.call-done), kind=kOutput, calls=%fused_computation.5 | convolution fusion | flops 14495514624 | bytes 41680896 | tf_op jit(solution)/shard_map/dot_general | solution.py:18
  442.2 35.0 %fusion.2 = f32[128,1536]{1,0:T(8,128)S(1)} fusion(f32[2,1536,6144]{2,1,0:T(8,128)} %param.6, f32[1,2,6144,128]{3,2,1,0:T(8,128)S(1)} %copy-done.4), kind=kOutput, calls=%fused_computation.7 | convolution fusion | flops 14495514624 | bytes 41680896 | tf_op jit(solution)/shard_map/dot_general | solution.py:18
  477.3 35.5 %fusion.97 = f32[1,1536,128]{1,2,0:T(8,128)S(1)} fusion(f32[128,1536]{1,0:T(8,128)S(1)} %fusion, f32[2,1536,6144]{2,1,0:T(8,128)} %param.6, f32[1,2,6144,128]{3,2,1,0:T(8,128)S(1)} %copy-done.4), kind=kOutput, calls=%fused_computation.87 | convolution fusion | flops 14495711232 | bytes 42467328 | tf_op jit(solution)/shard_map/dot_general | solution.py:18
  512.7 35.0 %fusion.91 = f32[1,1536,128]{1,2,0:T(8,128)S(1)} fusion(f32[128,1536]{1,0:T(8,128)S(1)} %fusion.2, f32[2,1536,6144]{2,1,0:T(8,128)} %param.6, f32[1,2,6144,128]{3,2,1,0:T(8,128)S(1)} %copy-done.4), kind=kOutput, calls=%fused_computation.85 | convolution fusion | flops 14495711232 | bytes 42467328 | tf_op jit(solution)/shard_map/dot_general | solution.py:18
  549.0 36.3 %fusion.12 = f32[128,1536]{1,0:T(8,128)S(1)} fusion(f32[2,1536,6144]{2,1,0:T(8,128)} %param.6, f32[1,2,6144,128]{3,2,1,0:T(8,128)} %all-gather.9.cloned.1.call-done), kind=kOutput, calls=%fused_computation.17 | convolution fusion | flops 14495514624 | bytes 41680896 | tf_op jit(solution)/shard_map/dot_general | solution.py:18
  585.3 35.0 %fusion.14 = f32[128,1536]{1,0:T(8,128)S(1)} fusion(f32[2,1536,6144]{2,1,0:T(8,128)} %param.6, f32[1,2,6144,128]{3,2,1,0:T(8,128)S(1)} %copy-done.5), kind=kOutput, calls=%fused_computation.19 | convolution fusion | flops 14495514624 | bytes 41680896 | tf_op jit(solution)/shard_map/dot_general | solution.py:18
  620.4 35.5 %fusion.61 = f32[1,1536,128]{1,2,0:T(8,128)S(1)} fusion(f32[128,1536]{1,0:T(8,128)S(1)} %fusion.12, f32[2,1536,6144]{2,1,0:T(8,128)} %param.6, f32[1,2,6144,128]{3,2,1,0:T(8,128)S(1)} %copy-done.5), kind=kOutput, calls=%fused_computation.75 | convolution fusion | flops 14495711232 | bytes 42467328 | tf_op jit(solution)/shard_map/dot_general | solution.py:18
  655.9 35.0 %fusion.55 = f32[1,1536,128]{1,2,0:T(8,128)S(1)} fusion(f32[128,1536]{1,0:T(8,128)S(1)} %fusion.14, f32[2,1536,6144]{2,1,0:T(8,128)} %param.6, f32[1,2,6144,128]{3,2,1,0:T(8,128)S(1)} %copy-done.5), kind=kOutput, calls=%fused_computation.73 | convolution fusion | flops 14495711232 | bytes 42467328 | tf_op jit(solution)/shard_map/dot_general | solution.py:18
  696.1 2.3 dynamic-slice_multiply_fusion
  698.4 2.5 dynamic-slice_multiply_fusion.3
  701.0 2.9 pad_maximum_fusion.1
  708.4 14.6 %all-reduce.12.cloned.1.call-done = (f32[2,1536,128]{1,2,0:T(8,128)}, f32[2,1536,128]{1,2,0:T(8,128)}, f32[2,1536,128]{1,2,0:T(8,128)}, f32[2,1536,128]{1,2,0:T(8,128)}) async-done(((f32[2,1536,128]{1,2,0:T(8,128)}, f32[2,1536,128]{1,2,0:T(8,128)}, f32[2,1536,128]{1,2,0:T(8,128)}, f32[2,1536,128]{1,2,0:T(8,128)}), (f32[2,1536,128]{1,2,0:T(8,128)}, f32[2,1536,128]{1,2,0:T(8,128)}, f32[2,1536,128]{1,2,0:T(8,128)}, ...) | async-done | bytes 6291472 | tf_op jit(solution)/shard_map/psum | solution.py:66
  732.7 3.3 fusion.220
  770.9 2.9 pad_maximum_fusion
  773.8 6.6 copy.33
  780.4 3.2 broadcast_in_dim.45
  783.6 13.1 %scatter_fusion = f32[4,2,1536,128]{3,2,1,0:T(8,128)} fusion(f32[4,2,1536,128]{3,2,1,0:T(8,128)} %broadcast_in_dim.45, s32[4]{0:T(128)S(1)} %copy-done.49, f32[4,2,1536,128]{3,2,1,0:T(8,128)} %copy.33), kind=kCustom, calls=%fused_computation.3 | custom fusion | bytes 18874384 | tf_op jit(solution)/shard_map/scatter | solution.py:118
  797.9 51.7 %all-reduce.6.cloned.1.call-done = f32[2,2,128,128]{3,2,1,0:T(8,128)} async-done(((f32[2,2,128,128]{3,2,1,0:T(8,128)}), f32[2,2,128,128]{3,2,1,0:T(8,128)}) %all-reduce.6.cloned.1.call-update) | async-done | bytes 262160 | tf_op jit(solution)/shard_map/psum | solution.py:102
  851.6 74.5 %all-reduce.8.cloned.1.call-done = f32[4,2,128,128]{3,2,1,0:T(8,128)} async-done(((f32[4,2,128,128]{3,2,1,0:T(8,128)}), f32[4,2,128,128]{3,2,1,0:T(8,128)}) %all-reduce.8.cloned.1.call-update) | async-done | bytes 524304 | tf_op jit(solution)/shard_map/psum | solution.py:104
  926.8 19.5 %all-reduce.10.cloned.1.call-done = f32[4,2,128,128]{3,2,1,0:T(8,128)} async-done(((f32[4,2,128,128]{3,2,1,0:T(8,128)}), f32[4,2,128,128]{3,2,1,0:T(8,128)}) %all-reduce.10.cloned.1.call-update) | async-done | bytes 524304 | tf_op jit(solution)/shard_map/psum | solution.py:104
  957.0 2.7 scatter_fusion.1
  (225 shorter events, 79.5 us)
Async XLA Ops:
  7.2 112.1 %all-gather.11.cloned.1.call-start = ((), (), s32[]{:S(2)}) async-start(), calls=%async_computation.4 | async-start | bytes 7077888 | tf_op jit(solution)/shard_map/all_gather | solution.py:64
  17.7 243.7 %all-gather.13.cloned.1.call-start = ((), (), s32[]{:S(2)}) async-start(), calls=%async_computation.5 | async-start | bytes 7077888 | tf_op jit(solution)/shard_map/all_gather | solution.py:64
  18.4 387.5 %all-gather.15.cloned.1.call-start = ((), (), s32[]{:S(2)}) async-start(), calls=%async_computation.6 | async-start | bytes 7077888 | tf_op jit(solution)/shard_map/all_gather | solution.py:64
  19.1 529.9 %all-gather.9.cloned.1.call-start = ((), (), s32[]{:S(2)}) async-start(), calls=%async_computation.3 | async-start | bytes 7077888 | tf_op jit(solution)/shard_map/all_gather | solution.py:64
  19.7 703.3 %all-reduce.12.cloned.1.call-start = ((), (), s32[]{:S(2)}) async-start(), calls=%async_computation.7 | async-start | bytes 12582912 | tf_op jit(solution)/shard_map/psum | solution.py:66
  119.2 36.1 %copy-start.2 = (f32[1,2,6144,128]{3,2,1,0:T(8,128)S(1)}, f32[1,2,6144,128]{3,2,1,0:T(8,128)}, u32[]{:S(2)}) copy-start(f32[1,2,6144,128]{3,2,1,0:T(8,128)} %all-gather.11.cloned.1.call-done) | copy-start | bytes 18874372
  261.3 36.6 %copy-start.3 = (f32[1,2,6144,128]{3,2,1,0:T(8,128)S(1)}, f32[1,2,6144,128]{3,2,1,0:T(8,128)}, u32[]{:S(2)}) copy-start(f32[1,2,6144,128]{3,2,1,0:T(8,128)} %all-gather.13.cloned.1.call-done) | copy-start | bytes 18874372
  405.9 36.3 %copy-start.4 = (f32[1,2,6144,128]{3,2,1,0:T(8,128)S(1)}, f32[1,2,6144,128]{3,2,1,0:T(8,128)}, u32[]{:S(2)}) copy-start(f32[1,2,6144,128]{3,2,1,0:T(8,128)} %all-gather.15.cloned.1.call-done) | copy-start | bytes 18874372
  549.0 36.3 %copy-start.5 = (f32[1,2,6144,128]{3,2,1,0:T(8,128)S(1)}, f32[1,2,6144,128]{3,2,1,0:T(8,128)}, u32[]{:S(2)}) copy-start(f32[1,2,6144,128]{3,2,1,0:T(8,128)} %all-gather.9.cloned.1.call-done) | copy-start | bytes 18874372
  692.2 157.4 %all-reduce.6.cloned.1.call-start = ((), (), s32[]{:S(2)}) async-start(), calls=%async_computation | async-start | bytes 524288 | tf_op jit(solution)/shard_map/psum | solution.py:102
  704.3 27.2 %collective-permute-start = (f32[4,2,1536,128]{3,2,1,0:T(8,128)}, f32[4,2,1536,128]{3,2,1,0:T(8,128)}, u32[]{:S(2)}, u32[]{:S(2)}) collective-permute-start(f32[4,2,1536,128]{3,2,1,0:T(8,128)} %pad_maximum_fusion.1), channel_id=1, source_target_pairs={{0,1},{1,0},{2,3},{3,2},{4,5},{5,4},{6,7},{7,6},{8,9},{9,8},{10,11... | collective-permute-start | bytes 18874376 | tf_op jit(solution)/shard_map/ppermute | solution.py:14
  725.2 15.1 %copy-start.23 = (f32[2,128,768]{2,1,0:T(8,128)}, f32[2,128,768]{2,1,0:T(8,128)S(1)}, u32[]{:S(2)}) copy-start(f32[2,128,768]{2,1,0:T(8,128)S(1)} %get-tuple-element.39) | copy-start | bytes 2359300
  725.2 28.1 %copy-start.21 = (f32[2,128,768]{2,1,0:T(8,128)}, f32[2,128,768]{2,1,0:T(8,128)S(1)}, u32[]{:S(2)}) copy-start(f32[2,128,768]{2,1,0:T(8,128)S(1)} %get-tuple-element.40) | copy-start | bytes 2359300
  736.4 16.9 %copy-start.18 = (f32[1,2,1536,128]{3,2,1,0:T(8,128)}, f32[1,2,1536,128]{3,2,1,0:T(8,128)S(1)}, u32[]{:S(2)}) copy-start(f32[1,2,1536,128]{3,2,1,0:T(8,128)S(1)} %get-tuple-element.13) | copy-start | bytes 4718596
  746.7 9.4 copy-start.6
  746.8 9.4 copy-start.8
  758.5 167.6 %all-reduce.8.cloned.1.call-start = ((), (), s32[]{:S(2)}) async-start(), calls=%async_computation.1 | async-start | bytes 1048576 | tf_op jit(solution)/shard_map/psum | solution.py:104
  758.6 9.9 %copy-start.19 = (f32[1,2,1536,128]{3,2,1,0:T(8,128)S(1)}, f32[1,2,1536,128]{3,2,1,0:T(8,128)}, u32[]{:S(2)}) copy-start(f32[1,2,1536,128]{3,2,1,0:T(8,128)} %copy-done.18) | copy-start | bytes 4718596
  758.6 9.9 %copy-start.22 = (f32[2,128,768]{2,1,0:T(8,128)S(1)}, f32[2,128,768]{2,1,0:T(8,128)}, u32[]{:S(2)}) copy-start(f32[2,128,768]{2,1,0:T(8,128)} %copy-done.21) | copy-start | bytes 2359300
  758.6 10.4 %copy-start.46 = (f32[128,128]{1,0:T(8,128)S(1)}, f32[128,128]{1,0:T(8,128)}, u32[]{:S(2)}) copy-start(f32[128,128]{1,0:T(8,128)} %fusion.130) | copy-start | bytes 196612
  783.6 13.1 %copy-start.43 = (f32[1,2,128,128]{3,2,1,0:T(8,128)S(1)}, f32[1,2,128,128]{3,2,1,0:T(8,128)}, u32[]{:S(2)}) copy-start(f32[1,2,128,128]{3,2,1,0:T(8,128)} %maximum_bitcast_fusion.5) | copy-start | bytes 393220
  783.6 13.1 %copy-start.44 = (f32[1,2,128,128]{3,2,1,0:T(8,128)S(1)}, f32[1,2,128,128]{3,2,1,0:T(8,128)}, u32[]{:S(2)}) copy-start(f32[1,2,128,128]{3,2,1,0:T(8,128)} %maximum_bitcast_fusion.4) | copy-start | bytes 393220
  783.6 65.9 %copy-start.32 = (f32[4,2,128,128]{3,2,1,0:T(8,128)S(1)}, f32[4,2,128,128]{3,2,1,0:T(8,128)}, u32[]{:S(2)}) copy-start(f32[4,2,128,128]{3,2,1,0:T(8,128)} %broadcast_select_fusion) | copy-start | bytes 1572868
  796.7 150.6 %copy-start.38 = (f32[2,128,128]{1,2,0:T(8,128)S(1)}, f32[2,128,128]{1,2,0:T(8,128)}, u32[]{:S(2)}) copy-start(f32[2,128,128]{1,2,0:T(8,128)} %get-tuple-element.29) | copy-start | bytes 393220
  796.7 151.3 %copy-start.37 = (f32[2,128,128]{1,2,0:T(8,128)S(1)}, f32[2,128,128]{1,2,0:T(8,128)}, u32[]{:S(2)}) copy-start(f32[2,128,128]{1,2,0:T(8,128)} %get-tuple-element.30) | copy-start | bytes 393220
  797.6 148.7 %all-reduce.10.cloned.1.call-start = ((), (), s32[]{:S(2)}) async-start(), calls=%async_computation.2 | async-start | bytes 1048576 | tf_op jit(solution)/shard_map/psum | solution.py:104
  850.6 76.2 %copy-start.33 = (f32[1,2,128,128]{3,2,1,0:T(8,128)}, f32[1,2,128,128]{3,2,1,0:T(8,128)S(1)}, u32[]{:S(2)}) copy-start(f32[1,2,128,128]{3,2,1,0:T(8,128)S(1)} %get-tuple-element.22) | copy-start | bytes 393220
  851.4 96.5 %copy-start.39 = (f32[128,128]{1,0:T(8,128)}, f32[128,128]{1,0:T(8,128)S(1)}, u32[]{:S(2)}) copy-start(f32[128,128]{1,0:T(8,128)S(1)} %convolution_add_fusion.5) | copy-start | bytes 196612
  851.6 96.3 %copy-start.40 = (f32[128,128]{1,0:T(8,128)}, f32[128,128]{1,0:T(8,128)S(1)}, u32[]{:S(2)}) copy-start(f32[128,128]{1,0:T(8,128)S(1)} %convolution_subtract_fusion.5) | copy-start | bytes 196612
  926.6 21.4 %copy-start.41 = (f32[128,128]{1,0:T(8,128)}, f32[128,128]{1,0:T(8,128)S(1)}, u32[]{:S(2)}) copy-start(f32[128,128]{1,0:T(8,128)S(1)} %convolution_add_fusion.3) | copy-start | bytes 196612
  926.8 21.5 %copy-start.42 = (f32[128,128]{1,0:T(8,128)}, f32[128,128]{1,0:T(8,128)S(1)}, u32[]{:S(2)}) copy-start(f32[128,128]{1,0:T(8,128)S(1)} %convolution_subtract_fusion.3) | copy-start | bytes 196612
  948.6 11.2 %copy-start.1 = (f32[4,2,768,128]{3,2,1,0:T(8,128)S(1)}, f32[4,2,768,128]{3,2,1,0:T(8,128)}, u32[]{:S(2)}) copy-start(f32[4,2,768,128]{3,2,1,0:T(8,128)} %param.7) | copy-start | bytes 9437188
  (33 other events, 162.6 us)
Sparse Core Ops, SparseCore 0:
  17.8 101.4 all-gather.10
  121.4 96.8 all-gather.12
  220.5 96.9 all-gather.14
  320.1 96.8 all-gather.8
  692.3 30.6 all-reduce.11
  758.7 90.8 all-reduce.5
  853.0 73.1 all-reduce.7
  928.5 17.7 all-reduce.9
